TPU v7x, 32 devices: a whole 2x2x4 slice. The times are simulated.
32 devices in a mesh: job: 2 (over x), tok: 16 (over z, y, core).
Axes of the slice: x: 2, y: 2, z: 4, core: 2. Of those that a mesh axis runs over, the one named last changes fastest.
Arguments:
- pair_states: bfloat16 [1024, 512, 128], P(('job', 'tok')), parts along dimension 0, may hold values from -6 to 6
- weight_in: bfloat16 [128, 1024], replicated, may hold values from -0.5 to 0.5
- weight_out: bfloat16 [512, 128], replicated, may hold values from -0.25 to 0.25
- weight_bias: bfloat16 [2, 128, 16], replicated, may hold values from -0.5 to 0.5
- key_mask: int32 [1024], P('job'), parts along dimension 0, may hold values 0 or 1
- noise_level: int32 [4], P('job'), parts along dimension 0, may hold values from 0 to 199
- query_states: bfloat16 [2, 16, 4, 48, 512], P(None, 'tok', 'job'), parts along dimension 2, may hold values from -16 to 16
- key_states: bfloat16 [2, 16, 4, 48, 512], P(None, 'tok', 'job'), parts along dimension 2, may hold values from -16 to 16
- value_states: bfloat16 [2, 16, 4, 48, 512], P(None, 'tok', 'job'), parts along dimension 2, may hold values from -6 to 6
- output_grad: bfloat16 [2, 16, 4, 48, 512], P(None, 'tok', 'job'), parts along dimension 2, may hold values from -6 to 6
Outputs:
- pair_grad: bfloat16 [1024, 512, 128], P(('job', 'tok')), parts along dimension 0
- query_grad: bfloat16 [2, 16, 4, 48, 512], P(None, 'tok', 'job'), parts along dimension 2
- key_grad: bfloat16 [2, 16, 4, 48, 512], P(None, 'tok', 'job'), parts along dimension 2
- value_grad: bfloat16 [2, 16, 4, 48, 512], P(None, 'tok', 'job'), parts along dimension 2
- weight_in_grad: float32 [256, 1024], P('job'), parts along dimension 0
- weight_out_grad: float32 [1024, 128], P('job'), parts along dimension 0
- weight_bias_grad: float32 [4, 128, 16], P('job'), parts along dimension 0
There are 2 independent parts, one for each index of `job`. A program takes and returns all parts, laid end to end along the dimension named above; an argument that names none is the same for every part. Nothing has to cross between parts.
All inputs are finite; a program needn't handle non-finite values.
Results may differ from a plain program's by a relative error of at most 0.015.
Values may be sent and summed in bfloat16 or wider, within the bound.
A program may use at most 192 MiB of HBM per device.

v0:
```python
import functools
import math

import jax
import jax.numpy as jnp
from jax import lax
from jax.experimental import pallas as pl
from jax.experimental.pallas import tpu as pltpu
from jax.sharding import PartitionSpec as P

LEVELS = 200
CHUNKS = 2
VMEM_LIMIT = 56 * 1024 * 1024

sigma_high = 160.0
sigma_low = 0.0004
sigma_data = 16.0
rho_power = 7.0
epsilon = 1e-05
masked_score = -1000000000.0

F32 = jnp.float32
BF16 = jnp.bfloat16


def sample_weight(levels):
    level = levels.astype(F32)
    top_root = sigma_high ** (1.0 / rho_power)
    low_root = sigma_low ** (1.0 / rho_power)
    sigma_level = (top_root + level / (LEVELS - 1) * (low_root - top_root)) ** rho_power
    return (sigma_level * sigma_level + sigma_data * sigma_data) / (sigma_level + sigma_data) ** 2


def normalize(inputs):
    row_mean = jnp.mean(inputs, -1, keepdims=True)
    centered = inputs - row_mean
    variance = jnp.mean(centered * centered, -1, keepdims=True)
    inv_std = lax.rsqrt(variance + epsilon)
    return (centered * inv_std, inv_std)


def norm_back(normed, inv_std, upstream):
    return inv_std * (
        upstream
        - jnp.mean(upstream, -1, keepdims=True)
        - normed * jnp.mean(upstream * normed, -1, keepdims=True)
    )


def mm(a, b, ca, cb):
    return lax.dot_general(a, b, (((ca,), (cb,)), ((), ())), preferred_element_type=F32)


def sigmoid(x):
    return 0.5 * jnp.tanh(0.5 * x) + 0.5


def forward_kernel(pair_ref, win_ref, wout_ref, wb_ref, bias_ref):
    width = wout_ref.shape[0]
    for r in range(pair_ref.shape[0]):
        pair_float = pair_ref[r].astype(F32)
        normed_in = normalize(pair_float)[0].astype(BF16)
        projected = mm(normed_in, win_ref[...], 1, 0)
        gate = projected[:, :width]
        hidden = (gate * sigmoid(gate) * projected[:, width:]).astype(BF16)
        lifted = pair_float + mm(hidden, wout_ref[...], 1, 0)
        normed_out = normalize(lifted)[0].astype(BF16)
        bias_ref[r] = mm(wb_ref[...], normed_out, 1, 1).astype(BF16)


def forward_rows(pair_states, win, wout, wb, chunk, chunks, step):
    rows, n, cz = pair_states.shape
    count = rows // chunks
    step = min(step, count)
    first = chunk * (count // step)
    heads = wb.shape[0]
    return pl.pallas_call(
        forward_kernel,
        name=f"pair_forward_{chunk}",
        grid=(count // step,),
        in_specs=[
            pl.BlockSpec((step, n, cz), lambda i: (first + i, 0, 0)),
            pl.BlockSpec(win.shape, lambda i: (0, 0)),
            pl.BlockSpec(wout.shape, lambda i: (0, 0)),
            pl.BlockSpec(wb.shape, lambda i: (0, 0)),
        ],
        out_specs=pl.BlockSpec((step, heads, n), lambda i: (i, 0, 0)),
        out_shape=jax.ShapeDtypeStruct((count, heads, n), BF16),
        compiler_params=pltpu.CompilerParams(vmem_limit_bytes=VMEM_LIMIT),
        cost_estimate=pl.CostEstimate(
            flops=2 * count * n * cz * (3 * wout.shape[0] + heads) * 2,
            bytes_accessed=count * n * (cz + heads) * 2,
            transcendentals=count * n * wout.shape[0],
        ),
    )(pair_states, win, wout, wb)


def backward_kernel(pair_ref, bias_ref, win_ref, wout_ref, wint_ref, woutt_ref, wb_ref, *rest):
    out_ref, acc_ref = rest[-2:]
    width = wout_ref.shape[0]
    heads = wb_ref.shape[0]

    @pl.when(pl.program_id(0) == 0)
    def _():
        if len(rest) == 4:
            acc_ref[...] = rest[0][...]
        else:
            acc_ref[...] = jnp.zeros_like(acc_ref)

    for r in range(pair_ref.shape[0]):
        pair_float = pair_ref[r].astype(F32)
        xhat, inv_in = normalize(pair_float)
        normed_in = xhat.astype(BF16)
        projected = mm(normed_in, win_ref[...], 1, 0)
        gate = projected[:, :width]
        up = projected[:, width:]
        sg = sigmoid(gate)
        act = gate * sg
        hidden = (act * up).astype(BF16)
        lifted = pair_float + mm(hidden, wout_ref[...], 1, 0)
        yhat, inv_out = normalize(lifted)
        normed_out = yhat.astype(BF16)
        bias = bias_ref[r]
        d_normed = mm(bias, wb_ref[...], 0, 0)
        d_lifted = norm_back(yhat, inv_out, d_normed)
        lifted_half = d_lifted.astype(BF16)
        d_hidden = mm(lifted_half, woutt_ref[...], 1, 0)
        d_gate = (d_hidden * up * (sg + act * (1.0 - sg))).astype(BF16)
        d_up = (d_hidden * act).astype(BF16)
        d_normed_in = mm(d_gate, wint_ref[:width], 1, 0) + mm(d_up, wint_ref[width:], 1, 0)
        out_ref[r] = (d_lifted + norm_back(xhat, inv_in, d_normed_in)).astype(BF16)
        acc_ref[:, :width] += mm(normed_in, d_gate, 0, 0)
        acc_ref[:, width : 2 * width] += mm(normed_in, d_up, 0, 0)
        acc_ref[:, 2 * width : 3 * width] += mm(lifted_half, hidden, 0, 0)
        acc_ref[:heads, 3 * width : 3 * width + pair_ref.shape[2]] += mm(bias, normed_out, 1, 0)


def backward_rows(pair_states, bias, win, wout, wb, previous, chunk, chunks, step):
    rows, n, cz = pair_states.shape
    width = wout.shape[0]
    heads = wb.shape[0]
    count = rows // chunks
    step = min(step, count)
    first = chunk * (count // step)
    columns = 3 * width + 2 * cz
    whole = lambda i: (0, 0)
    operands = [pair_states, bias, win, wout, win.T, wout.T, wb]
    specs = [
        pl.BlockSpec((step, n, cz), lambda i: (first + i, 0, 0)),
        pl.BlockSpec((step, heads, n), lambda i: (i, 0, 0)),
    ] + [pl.BlockSpec(a.shape, whole) for a in operands[2:]]
    aliases = {}
    if previous is not None:
        operands += [previous[1], previous[0]]
        specs += [pl.BlockSpec((cz, columns), whole), pl.BlockSpec(memory_space=pl.ANY)]
        aliases = {len(operands) - 1: 0}
    return pl.pallas_call(
        backward_kernel,
        name=f"pair_backward_{chunk}",
        grid=(count // step,),
        in_specs=specs,
        out_specs=[
            pl.BlockSpec((step, n, cz), lambda i: (first + i, 0, 0)),
            pl.BlockSpec((cz, columns), whole),
        ],
        out_shape=[
            jax.ShapeDtypeStruct(pair_states.shape, BF16),
            jax.ShapeDtypeStruct((cz, columns), F32),
        ],
        input_output_aliases=aliases,
        compiler_params=pltpu.CompilerParams(vmem_limit_bytes=VMEM_LIMIT),
        cost_estimate=pl.CostEstimate(
            flops=2 * count * n * cz * (9 * width + 2 * heads) * 2,
            bytes_accessed=count * n * (2 * cz + heads) * 2,
            transcendentals=count * n * width,
        ),
    )(*operands)


def attention_kernel(weight_ref, mask_ref, bias_ref, q_ref, k_ref, v_ref, g_ref,
                     dq_ref, dk_ref, dv_ref, sum_ref, total, att_buf, ds_buf, gh_buf):
    sample = pl.program_id(1)
    scaling = 1.0 / math.sqrt(q_ref.shape[0])
    n = q_ref.shape[1]
    tile = min(n, 128)
    gh_buf[...] = (weight_ref[sample] * g_ref[...].astype(F32)).astype(BF16)
    valid = mask_ref[...] > 0

    @pl.when(sample == 0)
    def _():
        total[...] = jnp.zeros_like(total)

    @pl.loop(0, n // tile)
    def _(i):
        rows = pl.ds(pl.multiple_of(i * tile, tile), tile)
        scores = mm(q_ref[:, rows], k_ref[...], 0, 0) * scaling + bias_ref[rows, :].astype(F32)
        scores = jnp.where(valid, scores, masked_score)
        peak = jnp.max(scores, -1, keepdims=True)
        powers = jnp.exp(scores - peak)
        attention = powers * (1.0 / jnp.sum(powers, -1, keepdims=True))
        att_buf[rows, :] = attention.astype(BF16)
        d_attention = mm(gh_buf[:, rows], v_ref[...], 0, 0)
        inner = jnp.sum(attention * d_attention, -1, keepdims=True)
        d_scores = attention * (d_attention - inner)
        ds_buf[rows, :] = d_scores.astype(BF16)
        total[rows, :] += d_scores

    dv_ref[...] = mm(gh_buf[...], att_buf[...], 1, 0).astype(BF16)
    dq_ref[...] = (mm(k_ref[...], ds_buf[...], 1, 1) * scaling).astype(BF16)
    dk_ref[...] = (mm(q_ref[...], ds_buf[...], 1, 0) * scaling).astype(BF16)

    @pl.when(sample == pl.num_programs(1) - 1)
    def _():
        sum_ref[...] = total[...].astype(BF16)


def attend(weights, mask, bias, queries, keys_in, values_in, grads_in):
    layers, _, samples, depth, n = queries.shape
    vec = pl.BlockSpec((None, None, None, depth, n), lambda b, s: (b, 0, s, 0, 0))
    grid_spec = pl.BlockSpec((None, n, n), lambda b, s: (b, 0, 0))
    return pl.pallas_call(
        attention_kernel,
        name="attention_back",
        grid=(layers, samples),
        in_specs=[
            pl.BlockSpec(memory_space=pltpu.SMEM),
            pl.BlockSpec((1, n), lambda b, s: (0, 0)),
            grid_spec, vec, vec, vec, vec,
        ],
        out_specs=[vec, vec, vec, grid_spec],
        out_shape=[jax.ShapeDtypeStruct(queries.shape, BF16)] * 3
        + [jax.ShapeDtypeStruct((layers, n, n), BF16)],
        scratch_shapes=[
            pltpu.VMEM((n, n), F32),
            pltpu.VMEM((n, n), BF16),
            pltpu.VMEM((n, n), BF16),
            pltpu.VMEM((depth, n), BF16),
        ],
        compiler_params=pltpu.CompilerParams(vmem_limit_bytes=VMEM_LIMIT),
    )(weights, mask, bias, queries, keys_in, values_in, grads_in)


PIECES = 16


def reduce_kernel(devices, part_ref, out_ref, acc, sent, got, full, send_sem, recv_sem, pass_sem, land_sem):
    me = lax.axis_index("tok")
    stages = devices.bit_length() - 1
    half_rows = PIECES // 2
    piece_rows = part_ref.shape[0] // half_rows
    piece_columns = part_ref.shape[1] // 2
    bits = [lax.rem(me // (1 << k), 2) for k in range(stages)]
    partners = [me + (1 - 2 * bits[k]) * (1 << k) for k in range(stages)]
    barrier = pltpu.get_barrier_semaphore()
    for partner in partners:
        pl.semaphore_signal(
            barrier, inc=1, device_id={"tok": partner}, device_id_type=pl.DeviceIdType.MESH
        )
    for half in range(2):
        for band in range(half_rows):
            acc[half * half_rows + band] = part_ref[
                band * piece_rows : (band + 1) * piece_rows,
                half * piece_columns : (half + 1) * piece_columns,
            ]
    pl.semaphore_wait(barrier, stages)

    low = 0
    length = PIECES
    used = 0
    spans = []
    for k in range(stages):
        split = length > 1
        size = length // 2 if split else 1
        away = low + (1 - bits[k]) * size if split else low
        low = low + bits[k] * size if split else low
        sent[used : used + size] = acc[pl.ds(away, size)].astype(BF16)
        copy = pltpu.make_async_remote_copy(
            src_ref=sent.at[pl.ds(used, size)],
            dst_ref=got.at[pl.ds(used, size)],
            send_sem=send_sem.at[k],
            recv_sem=recv_sem.at[k],
            device_id={"tok": partners[k]},
            device_id_type=pl.DeviceIdType.MESH,
        )
        copy.start()
        copy.wait()
        if split:
            acc[pl.ds(low, size)] = acc[pl.ds(low, size)] + got[used : used + size].astype(F32)
            spans.append((k, low, size))
        else:
            acc[pl.ds(low, size)] = sent[used : used + size].astype(F32) + got[
                used : used + size
            ].astype(F32)
        length = size
        used += size

    full[pl.ds(low, length)] = acc[pl.ds(low, length)].astype(BF16)
    for k, start, size in reversed(spans):
        copy = pltpu.make_async_remote_copy(
            src_ref=full.at[pl.ds(start, size)],
            dst_ref=full.at[pl.ds(start, size)],
            send_sem=pass_sem.at[k],
            recv_sem=land_sem.at[k],
            device_id={"tok": partners[k]},
            device_id_type=pl.DeviceIdType.MESH,
        )
        copy.start()
        copy.wait()
    for half in range(2):
        for band in range(half_rows):
            out_ref[
                band * piece_rows : (band + 1) * piece_rows,
                half * piece_columns : (half + 1) * piece_columns,
            ] = full[half * half_rows + band].astype(F32)


def reduce_all(part, devices):
    rows, columns = part.shape
    stages = devices.bit_length() - 1
    piece = (rows // (PIECES // 2), columns // 2)
    slots = 0
    length = PIECES
    for _ in range(stages):
        length = max(length // 2, 1)
        slots += length
    dma = pltpu.SemaphoreType.DMA((stages,))
    return pl.pallas_call(
        functools.partial(reduce_kernel, devices),
        name="weight_reduce",
        in_specs=[pl.BlockSpec(memory_space=pltpu.VMEM)],
        out_specs=pl.BlockSpec(memory_space=pltpu.VMEM),
        out_shape=jax.ShapeDtypeStruct(part.shape, F32),
        scratch_shapes=[
            pltpu.VMEM((PIECES,) + piece, F32),
            pltpu.VMEM((slots,) + piece, BF16),
            pltpu.VMEM((slots,) + piece, BF16),
            pltpu.VMEM((PIECES,) + piece, BF16),
            dma, dma, dma, dma,
        ],
        compiler_params=pltpu.CompilerParams(
            collective_id=0, has_side_effects=True, vmem_limit_bytes=VMEM_LIMIT
        ),
    )(part)


def exchange(x):
    return lax.all_to_all(x, "tok", split_axis=0, concat_axis=0, tiled=True)


def body(
    pair_states,
    weight_in,
    weight_out,
    weight_bias,
    key_mask,
    noise_level,
    query_states,
    key_states,
    value_states,
    output_grad,
):
    rows, n, cz = pair_states.shape
    layers, _, head_count = weight_bias.shape
    width = weight_out.shape[0]
    devices = lax.axis_size("tok")
    groups = devices // head_count
    samples = query_states.shape[2]
    chunks = CHUNKS if rows % CHUNKS == 0 else 1
    part = rows // chunks
    heads = head_count * layers
    wb = jnp.transpose(weight_bias, (2, 0, 1)).reshape(heads, cz)

    arrived = []
    for chunk in range(chunks):
        tiles = forward_rows(pair_states, weight_in, weight_out, wb, chunk, chunks, 2)
        tiles = tiles.reshape(part, head_count, layers, n).transpose(1, 2, 0, 3)
        arrived.append(exchange(jnp.tile(tiles, (groups, 1, 1, 1))))
    bias = jnp.stack(arrived, 2)
    bias = bias.transpose(1, 0, 2, 3, 4).reshape(layers, n, n)

    group = lax.axis_index("tok") // head_count
    weights = sample_weight(lax.dynamic_slice_in_dim(noise_level, group * samples, samples))
    query_grad, key_grad, value_grad, sums = attend(
        weights, key_mask.reshape(1, n), bias,
        query_states, key_states, value_states, output_grad,
    )
    totals = sums.reshape(layers, devices, chunks, part, n)
    returned = [exchange(totals[:, :, chunk].transpose(1, 0, 2, 3)) for chunk in range(chunks)]
    state = None
    for chunk in range(chunks):
        back = returned[chunk]
        if groups > 1:
            back = back.reshape(groups, heads, part, n).astype(F32).sum(0).astype(BF16)
        back = back.reshape(heads, part, n).transpose(1, 0, 2)
        state = backward_rows(
            pair_states, back, weight_in, weight_out, wb, state, chunk, chunks, 2
        )
    pair_grad, acc = state
    acc = reduce_all(acc, devices)
    grad_in = acc[:, : 2 * width]
    grad_out = acc[:, 2 * width : 3 * width].T
    grad_bias = acc[:heads, 3 * width : 3 * width + cz].reshape(head_count, layers, cz)
    grad_bias = grad_bias.transpose(1, 2, 0)
    return (pair_grad, query_grad, key_grad, value_grad, grad_in, grad_out, grad_bias)


def solution(mesh):
    in_specs = (
        P(("job", "tok"), None, None),
        P(),
        P(),
        P(),
        P("job"),
        P("job"),
        P(None, "tok", "job", None, None),
        P(None, "tok", "job", None, None),
        P(None, "tok", "job", None, None),
        P(None, "tok", "job", None, None),
    )
    out_specs = (
        P(("job", "tok"), None, None),
        P(None, "tok", "job", None, None),
        P(None, "tok", "job", None, None),
        P(None, "tok", "job", None, None),
        P("job", None),
        P("job", None),
        P("job", None, None),
    )
    return jax.shard_map(body, mesh=mesh, in_specs=in_specs, out_specs=out_specs, check_vma=False)
```

profile of v0, /device:TPU:0, one launch (start us, length us, event | category | flops | bytes accessed | tf_op | source)
XLA Modules:
  0.0 223.0 jit_solution(6319854574863706091)
XLA Ops:
  0.6 1.3 copy.27
  1.9 18.3 %pair_forward_1.1 = bf16[16,32,512]{2,1,0:T(8,128)(2,1)} custom-call(bf16[32,512,128]{2,1,0:T(8,128)(2,1)} %pair_ref.7, bf16[128,1024]{1,0:T(8,128)(2,1)} %win_ref.7, bf16[512,128]{1,0:T(8,128)(2,1)} %wout_ref.7, bf16[32,128]{1,0:T(8,128)(2,1)} %bitcast.52), custom_call_target="tpu_custom_call" | custom-call | flops 6576668672 | bytes 2621440 | tf_op jit(solution)/shard_map/pair_forward_1/pallas_call | solution.py:77
  20.3 2.1 copy.40
  22.4 7.4 %all-to-all-start.1 = ((bf16[16,2,16,512]{3,2,1,0:T(8,128)(2,1)}), bf16[16,2,16,512]{3,2,1,0:T(8,128)(2,1)S(1)}, u32[]{:S(2)}, u32[]{:S(2)}) async-start(bf16[16,2,16,512]{3,2,1,0:T(8,128)(2,1)} %bitcast.7), calls=%async_computation.1 | async-start | bytes 1048576 | tf_op jit(solution)/shard_map/all_to_all | solution.py:347
  29.8 0.0 copy-start.2
  29.8 18.4 %pair_forward_0.1 = bf16[16,32,512]{2,1,0:T(8,128)(2,1)} custom-call(bf16[32,512,128]{2,1,0:T(8,128)(2,1)} %pair_ref.7, bf16[128,1024]{1,0:T(8,128)(2,1)} %win_ref.7, bf16[512,128]{1,0:T(8,128)(2,1)} %wout_ref.7, bf16[32,128]{1,0:T(8,128)(2,1)} %bitcast.53), custom_call_target="tpu_custom_call" | custom-call | flops 6576668672 | bytes 2621440 | tf_op jit(solution)/shard_map/pair_forward_0/pallas_call | solution.py:77
  48.2 2.1 copy.39
  50.4 0.0 all-to-all-done.1
  50.4 6.0 %all-to-all-start = ((bf16[16,2,16,512]{3,2,1,0:T(8,128)(2,1)}), bf16[16,2,16,512]{3,2,1,0:T(8,128)(2,1)S(1)}, u32[]{:S(2)}, u32[]{:S(2)}) async-start(bf16[16,2,16,512]{3,2,1,0:T(8,128)(2,1)} %bitcast.4), calls=%async_computation | async-start | bytes 1048576 | tf_op jit(solution)/shard_map/all_to_all | solution.py:347
  56.4 0.0 copy-done.2
  56.4 0.5 multiply_divide_fusion.weight_ref
  56.9 13.7 %all-to-all-done = bf16[16,2,16,512]{3,2,1,0:T(8,128)(2,1)S(1)} async-done(((bf16[16,2,16,512]{3,2,1,0:T(8,128)(2,1)}), bf16[16,2,16,512]{3,2,1,0:T(8,128)(2,1)S(1)}, u32[]{:S(2)}, u32[]{:S(2)}) %all-to-all-start) | async-done | bytes 524320 | tf_op jit(solution)/shard_map/all_to_all | solution.py:347
  70.6 0.1 maximum_bitcast_fusion
  70.7 1.1 copy.30
  71.8 0.0 copy-start.1
  71.8 0.0 copy-start
  71.8 12.0 %attention_back.1 = (bf16[2,1,2,48,512]{4,3,2,1,0:T(8,128)(2,1)}, bf16[2,1,2,48,512]{4,3,2,1,0:T(8,128)(2,1)}, bf16[2,1,2,48,512]{4,3,2,1,0:T(8,128)(2,1)}, bf16[2,512,512]{2,1,0:T(8,128)(2,1)}) custom-call(f32[2]{0:T(128)} %multiply_divide_fusion.weight_ref, s32[1,512]{1,0:T(1,128)} %bitcast.56, bf16[2,512,512]{2,1,0:T(8,128)(2,1)} %bitcast.39, ...), custom_call_target="tpu_custom_call" | custom-call | tf_op jit(solution)/shard_map/attention_back/pallas_call | solution.py:221
  83.8 1.3 fusion
  85.1 1.3 copy.46
  86.5 4.2 %all-to-all-start.3 = ((bf16[16,2,16,512]{3,1,2,0:T(2,128)(2,1)}), bf16[16,2,16,512]{3,1,2,0:T(2,128)(2,1)S(1)}, u32[]{:S(2)}, u32[]{:S(2)}) async-start(bf16[16,2,16,512]{3,1,2,0:T(2,128)(2,1)} %bitcast.36), calls=%async_computation.3 | async-start | bytes 1048576 | tf_op jit(solution)/shard_map/all_to_all | solution.py:347
  90.6 1.3 copy.47
  92.0 12.9 %all-to-all-done.3 = bf16[16,2,16,512]{3,1,2,0:T(2,128)(2,1)S(1)} async-done(((bf16[16,2,16,512]{3,1,2,0:T(2,128)(2,1)}), bf16[16,2,16,512]{3,1,2,0:T(2,128)(2,1)S(1)}, u32[]{:S(2)}, u32[]{:S(2)}) %all-to-all-start.3) | async-done | bytes 524320 | tf_op jit(solution)/shard_map/all_to_all | solution.py:347
  104.9 4.2 %all-to-all-start.2 = ((bf16[16,2,16,512]{3,1,2,0:T(2,128)(2,1)}), bf16[16,2,16,512]{3,1,2,0:T(2,128)(2,1)S(1)}, u32[]{:S(2)}, u32[]{:S(2)}) async-start(bf16[16,2,16,512]{3,1,2,0:T(2,128)(2,1)} %bitcast.37), calls=%async_computation.2 | async-start | bytes 1048576 | tf_op jit(solution)/shard_map/all_to_all | solution.py:347
  109.1 0.0 copy-done.1
  109.1 0.8 copy.34
  109.9 0.0 copy-done
  109.9 0.8 copy.33
  110.7 0.5 copy.36
  111.2 1.0 reshape.48
  112.2 11.1 %all-to-all-done.2 = bf16[16,2,16,512]{3,1,2,0:T(2,128)(2,1)S(1)} async-done(((bf16[16,2,16,512]{3,1,2,0:T(2,128)(2,1)}), bf16[16,2,16,512]{3,1,2,0:T(2,128)(2,1)S(1)}, u32[]{:S(2)}, u32[]{:S(2)}) %all-to-all-start.2) | async-done | bytes 524320 | tf_op jit(solution)/shard_map/all_to_all | solution.py:347
  123.3 0.5 copy.32
  123.8 1.0 reshape.47
  124.8 32.0 %pair_backward_0.1 = (bf16[32,512,128]{2,1,0:T(8,128)(2,1)}, f32[128,1792]{1,0:T(8,128)}) custom-call(bf16[32,512,128]{2,1,0:T(8,128)(2,1)} %pair_ref.7, bf16[16,32,512]{2,1,0:T(8,128)(2,1)} %bitcast.43, bf16[128,1024]{1,0:T(8,128)(2,1)} %win_ref.7, bf16[512,128]{1,0:T(8,128)(2,1)} %wout_ref.7, bf16[1024,128]{1,0:T(8,128)(2,1)} %bitcast.45, ...), custom_call_target="tpu_custom_call" | custom-call | flops 19595788288 | bytes 4718592 | tf_op jit(solution)/shard_map/pair_backward_0/pallas_call | solution.py:157
  156.8 32.5 %pair_backward_1.1 = (bf16[32,512,128]{2,1,0:T(8,128)(2,1)}, f32[128,1792]{1,0:T(8,128)}) custom-call(bf16[32,512,128]{2,1,0:T(8,128)(2,1)} %pair_ref.7, bf16[16,32,512]{2,1,0:T(8,128)(2,1)} %bitcast.44, bf16[128,1024]{1,0:T(8,128)(2,1)} %win_ref.7, bf16[512,128]{1,0:T(8,128)(2,1)} %wout_ref.7, ...), custom_call_target="tpu_custom_call", output_to_operand_aliasing={{0}: (8, {})} | custom-call | flops 19595788288 | bytes 4718592 | tf_op jit(solution)/shard_map/pair_backward_1/pallas_call | solution.py:157
  189.3 28.7 %weight_reduce.1 = f32[128,1792]{1,0:T(8,128)} custom-call(f32[128,1792]{1,0:T(8,128)} %get-tuple-element.22.part_ref), custom_call_target="tpu_custom_call" | custom-call | tf_op jit(solution)/shard_map/weight_reduce/pallas_call | solution.py:327
  218.0 0.7 slice.19
  218.7 1.0 slice_bitcast_fusion
  219.7 1.9 slice.17
  221.6 0.6 copy.48
  222.2 0.8 copy.38
Async XLA Ops:
  22.4 28.0 %all-to-all-start.1 = ((bf16[16,2,16,512]{3,2,1,0:T(8,128)(2,1)}), bf16[16,2,16,512]{3,2,1,0:T(8,128)(2,1)S(1)}, u32[]{:S(2)}, u32[]{:S(2)}) async-start(bf16[16,2,16,512]{3,2,1,0:T(8,128)(2,1)} %bitcast.7), calls=%async_computation.1 | async-start | bytes 1048576 | tf_op jit(solution)/shard_map/all_to_all | solution.py:347
  29.8 26.5 %copy-start.2 = (s32[2]{0:T(128)S(1)}, s32[2]{0:T(128)}, u32[]{:S(2)}) copy-start(s32[2]{0:T(128)} %param.15) | copy-start | bytes 28
  50.4 20.3 %all-to-all-start = ((bf16[16,2,16,512]{3,2,1,0:T(8,128)(2,1)}), bf16[16,2,16,512]{3,2,1,0:T(8,128)(2,1)S(1)}, u32[]{:S(2)}, u32[]{:S(2)}) async-start(bf16[16,2,16,512]{3,2,1,0:T(8,128)(2,1)} %bitcast.4), calls=%async_computation | async-start | bytes 1048576 | tf_op jit(solution)/shard_map/all_to_all | solution.py:347
  71.8 37.3 %copy-start.1 = (bf16[512,128]{1,0:T(8,128)(2,1)S(1)}, bf16[512,128]{1,0:T(8,128)(2,1)}, u32[]{:S(2)}) copy-start(bf16[512,128]{1,0:T(8,128)(2,1)} %wout_ref.7) | copy-start | bytes 393220
  71.8 38.1 %copy-start = (bf16[128,1024]{1,0:T(8,128)(2,1)S(1)}, bf16[128,1024]{1,0:T(8,128)(2,1)}, u32[]{:S(2)}) copy-start(bf16[128,1024]{1,0:T(8,128)(2,1)} %win_ref.7) | copy-start | bytes 786436
  86.5 18.4 %all-to-all-start.3 = ((bf16[16,2,16,512]{3,1,2,0:T(2,128)(2,1)}), bf16[16,2,16,512]{3,1,2,0:T(2,128)(2,1)S(1)}, u32[]{:S(2)}, u32[]{:S(2)}) async-start(bf16[16,2,16,512]{3,1,2,0:T(2,128)(2,1)} %bitcast.36), calls=%async_computation.3 | async-start | bytes 1048576 | tf_op jit(solution)/shard_map/all_to_all | solution.py:347
  104.9 18.4 %all-to-all-start.2 = ((bf16[16,2,16,512]{3,1,2,0:T(2,128)(2,1)}), bf16[16,2,16,512]{3,1,2,0:T(2,128)(2,1)S(1)}, u32[]{:S(2)}, u32[]{:S(2)}) async-start(bf16[16,2,16,512]{3,1,2,0:T(2,128)(2,1)} %bitcast.37), calls=%async_computation.2 | async-start | bytes 1048576 | tf_op jit(solution)/shard_map/all_to_all | solution.py:347
where the time goes:
time: 224 us; the launch traced here: 223 us
  Pallas kernels  142 us (63%)
  waiting for transfers between devices  37.8 us (17%)
  starting transfers between devices  21.7 us (10%)
  local copies, waits for them, and re-layouts  20.2 us (9%)
    pallas_call x2, Pallas kernels, backward_rows(): pl.pallas_call(backward_kernel, name=f'pair_backward_{chunk}', grid=(coun...  64.4 us
    all_to_all x4, waiting for transfers between devices, exchange(): return lax.all_to_all(x, 'tok', split_axis=0, concat_axis=0, tiled=True)  37.8 us
    pallas_call x2, Pallas kernels, forward_rows(): pl.pallas_call(forward_kernel, name=f'pair_forward_{chunk}', grid=(count...  36.7 us
    pallas_call x1, Pallas kernels, reduce_all(): pl.pallas_call(functools.partial(reduce_kernel, devices), name='weight_re...  28.7 us
    all_to_all x4, starting transfers between devices, exchange(): return lax.all_to_all(x, 'tok', split_axis=0, concat_axis=0, tiled=True)  21.7 us
    pallas_call x1, Pallas kernels, attend(): pl.pallas_call(attention_kernel, name='attention_back', grid=(layers, sam...  12 us
    unnamed x11, local copies, waits for them, and re-layouts  5.14 us
  transfers between devices with their start and end apart: 4, of which 3 were waited for; matrix products, arithmetic and copies ran while one was open for 3% of the time, Pallas kernels for 8%

commit v1 on v0

--- a/solution.py
+++ b/solution.py
@@ -385,7 +385,12 @@
         query_states, key_states, value_states, output_grad,
     )
     totals = sums.reshape(layers, devices, chunks, part, n)
-    returned = [exchange(totals[:, :, chunk].transpose(1, 0, 2, 3)) for chunk in range(chunks)]
+    returned = []
+    for chunk in range(chunks):
+        outgoing = totals[:, :, chunk].transpose(1, 0, 2, 3)
+        if returned:
+            returned[-1], outgoing = lax.optimization_barrier((returned[-1], outgoing))
+        returned.append(exchange(outgoing))
     state = None
     for chunk in range(chunks):
         back = returned[chunk]

time: 224 us -> 212 us (0.946)
  waiting for transfers between devices: 37.8 us -> 25 us
    all_to_all x4, waiting for transfers between devices: 37.8 us -> 25 us  [exchange(): return lax.all_to_all(x, 'tok', split_axis=0, concat_axis=0, tiled=True)]
  transfers between devices with their start and end apart: 4 -> 4, of which waited for: 3 -> 2; matrix products, arithmetic and copies ran while one was open for 3% -> 3% of each run, Pallas kernels for 8% -> 24%
where the time goes in v1:
time: 212 us; the launch traced here: 211 us
  Pallas kernels  142 us (67%)
  waiting for transfers between devices  25 us (12%)
  starting transfers between devices  21.7 us (10%)
  local copies, waits for them, and re-layouts  20.2 us (10%)
    pallas_call x2, Pallas kernels, backward_rows(): pl.pallas_call(backward_kernel, name=f'pair_backward_{chunk}', grid=(coun...  64.4 us
    pallas_call x2, Pallas kernels, forward_rows(): pl.pallas_call(forward_kernel, name=f'pair_forward_{chunk}', grid=(count...  36.7 us
    pallas_call x1, Pallas kernels, reduce_all(): pl.pallas_call(functools.partial(reduce_kernel, devices), name='weight_re...  29.2 us
    all_to_all x4, waiting for transfers between devices, exchange(): return lax.all_to_all(x, 'tok', split_axis=0, concat_axis=0, tiled=True)  25 us
    all_to_all x4, starting transfers between devices, exchange(): return lax.all_to_all(x, 'tok', split_axis=0, concat_axis=0, tiled=True)  21.7 us
    pallas_call x1, Pallas kernels, attend(): pl.pallas_call(attention_kernel, name='attention_back', grid=(layers, sam...  11.9 us
    unnamed x11, local copies, waits for them, and re-layouts  5.15 us
    reshape x2, local copies, waits for them, and re-layouts, body(): tiles = tiles.reshape(part, head_count, layers, n).transpose(1, 2, 0, 3)  4.25 us
  transfers between devices with their start and end apart: 4, of which 2 were waited for; matrix products, arithmetic and copies ran while one was open for 3% of the time, Pallas kernels for 24%

profile of v1, /device:TPU:0, one launch (start us, length us, event | category | flops | bytes accessed | tf_op | source)
XLA Modules:
  0.0 210.6 jit_solution(4202347126483865477)
XLA Ops:
  0.6 1.3 copy.27
  1.9 18.3 %pair_forward_1.1 = bf16[16,32,512]{2,1,0:T(8,128)(2,1)} custom-call(bf16[32,512,128]{2,1,0:T(8,128)(2,1)} %pair_ref.7, bf16[128,1024]{1,0:T(8,128)(2,1)} %win_ref.7, bf16[512,128]{1,0:T(8,128)(2,1)} %wout_ref.7, bf16[32,128]{1,0:T(8,128)(2,1)} %bitcast.52), custom_call_target="tpu_custom_call" | custom-call | flops 6576668672 | bytes 2621440 | tf_op jit(solution)/shard_map/pair_forward_1/pallas_call | solution.py:77
  20.3 2.1 %copy.40 = bf16[16,32,512]{2,0,1:T(8,128)(2,1)} copy(bf16[16,32,512]{2,1,0:T(8,128)(2,1)} %pair_forward_1.1) | data formatting | bytes 1048576 | tf_op jit(solution)/shard_map/reshape | solution.py:376
  22.4 7.4 %all-to-all-start.1 = ((bf16[16,2,16,512]{3,2,1,0:T(8,128)(2,1)}), bf16[16,2,16,512]{3,2,1,0:T(8,128)(2,1)S(1)}, u32[]{:S(2)}, u32[]{:S(2)}) async-start(bf16[16,2,16,512]{3,2,1,0:T(8,128)(2,1)} %bitcast.7), calls=%async_computation.1 | async-start | bytes 1048576 | tf_op jit(solution)/shard_map/all_to_all | solution.py:347
  29.8 0.0 copy-start.2
  29.8 18.4 %pair_forward_0.1 = bf16[16,32,512]{2,1,0:T(8,128)(2,1)} custom-call(bf16[32,512,128]{2,1,0:T(8,128)(2,1)} %pair_ref.7, bf16[128,1024]{1,0:T(8,128)(2,1)} %win_ref.7, bf16[512,128]{1,0:T(8,128)(2,1)} %wout_ref.7, bf16[32,128]{1,0:T(8,128)(2,1)} %bitcast.53), custom_call_target="tpu_custom_call" | custom-call | flops 6576668672 | bytes 2621440 | tf_op jit(solution)/shard_map/pair_forward_0/pallas_call | solution.py:77
  48.2 2.1 %copy.39 = bf16[16,32,512]{2,0,1:T(8,128)(2,1)} copy(bf16[16,32,512]{2,1,0:T(8,128)(2,1)} %pair_forward_0.1) | data formatting | bytes 1048576 | tf_op jit(solution)/shard_map/reshape | solution.py:376
  50.4 0.0 all-to-all-done.1
  50.4 6.0 %all-to-all-start = ((bf16[16,2,16,512]{3,2,1,0:T(8,128)(2,1)}), bf16[16,2,16,512]{3,2,1,0:T(8,128)(2,1)S(1)}, u32[]{:S(2)}, u32[]{:S(2)}) async-start(bf16[16,2,16,512]{3,2,1,0:T(8,128)(2,1)} %bitcast.4), calls=%async_computation | async-start | bytes 1048576 | tf_op jit(solution)/shard_map/all_to_all | solution.py:347
  56.4 0.0 copy-done.2
  56.4 0.5 multiply_divide_fusion.weight_ref
  56.9 13.7 %all-to-all-done = bf16[16,2,16,512]{3,2,1,0:T(8,128)(2,1)S(1)} async-done(((bf16[16,2,16,512]{3,2,1,0:T(8,128)(2,1)}), bf16[16,2,16,512]{3,2,1,0:T(8,128)(2,1)S(1)}, u32[]{:S(2)}, u32[]{:S(2)}) %all-to-all-start) | async-done | bytes 524320 | tf_op jit(solution)/shard_map/all_to_all | solution.py:347
  70.6 0.1 maximum_bitcast_fusion
  70.7 0.0 copy-start.1
  70.7 0.0 copy-start
  70.8 1.1 copy.30
  71.8 11.9 %attention_back.1 = (bf16[2,1,2,48,512]{4,3,2,1,0:T(8,128)(2,1)}, bf16[2,1,2,48,512]{4,3,2,1,0:T(8,128)(2,1)}, bf16[2,1,2,48,512]{4,3,2,1,0:T(8,128)(2,1)}, bf16[2,512,512]{2,1,0:T(8,128)(2,1)}) custom-call(f32[2]{0:T(128)} %multiply_divide_fusion.weight_ref, s32[1,512]{1,0:T(1,128)} %bitcast.56, bf16[2,512,512]{2,1,0:T(8,128)(2,1)} %bitcast.39, ...), custom_call_target="tpu_custom_call" | custom-call | tf_op jit(solution)/shard_map/attention_back/pallas_call | solution.py:221
  83.7 1.3 fusion
  85.0 1.3 copy.47
  86.3 4.2 %all-to-all-start.2 = ((bf16[16,2,16,512]{3,1,2,0:T(2,128)(2,1)}), bf16[16,2,16,512]{3,1,2,0:T(2,128)(2,1)S(1)}, u32[]{:S(2)}, u32[]{:S(2)}) async-start(bf16[16,2,16,512]{3,1,2,0:T(2,128)(2,1)} %bitcast.37), calls=%async_computation.2 | async-start | bytes 1048576 | tf_op jit(solution)/shard_map/all_to_all | solution.py:347
  90.5 0.0 copy-done.1
  90.5 0.8 copy.35
  91.3 0.0 copy-done
  91.3 0.8 copy.34
  92.2 1.3 copy.46
  93.5 11.3 %all-to-all-done.2 = bf16[16,2,16,512]{3,1,2,0:T(2,128)(2,1)S(1)} async-done(((bf16[16,2,16,512]{3,1,2,0:T(2,128)(2,1)}), bf16[16,2,16,512]{3,1,2,0:T(2,128)(2,1)S(1)}, u32[]{:S(2)}, u32[]{:S(2)}) %all-to-all-start.2) | async-done | bytes 524320 | tf_op jit(solution)/shard_map/all_to_all | solution.py:347
  104.8 4.2 %all-to-all-start.3 = ((bf16[16,2,16,512]{3,1,2,0:T(2,128)(2,1)}), bf16[16,2,16,512]{3,1,2,0:T(2,128)(2,1)S(1)}, u32[]{:S(2)}, u32[]{:S(2)}) async-start(bf16[16,2,16,512]{3,1,2,0:T(2,128)(2,1)} %bitcast.36), calls=%async_computation.3 | async-start | bytes 1048576 | tf_op jit(solution)/shard_map/all_to_all | solution.py:347
  109.0 0.5 copy.36
  109.5 1.0 reshape.48
  110.5 32.0 %pair_backward_0.1 = (bf16[32,512,128]{2,1,0:T(8,128)(2,1)}, f32[128,1792]{1,0:T(8,128)}) custom-call(bf16[32,512,128]{2,1,0:T(8,128)(2,1)} %pair_ref.7, bf16[16,32,512]{2,1,0:T(8,128)(2,1)} %bitcast.44, bf16[128,1024]{1,0:T(8,128)(2,1)} %win_ref.7, bf16[512,128]{1,0:T(8,128)(2,1)} %wout_ref.7, bf16[1024,128]{1,0:T(8,128)(2,1)} %bitcast.45, ...), custom_call_target="tpu_custom_call" | custom-call | flops 19595788288 | bytes 4718592 | tf_op jit(solution)/shard_map/pair_backward_0/pallas_call | solution.py:157
  142.5 0.0 all-to-all-done.3
  142.5 0.5 copy.33
  143.0 1.0 reshape.47
  144.0 32.4 %pair_backward_1.1 = (bf16[32,512,128]{2,1,0:T(8,128)(2,1)}, f32[128,1792]{1,0:T(8,128)}) custom-call(bf16[32,512,128]{2,1,0:T(8,128)(2,1)} %pair_ref.7, bf16[16,32,512]{2,1,0:T(8,128)(2,1)} %bitcast.43, bf16[128,1024]{1,0:T(8,128)(2,1)} %win_ref.7, bf16[512,128]{1,0:T(8,128)(2,1)} %wout_ref.7, ...), custom_call_target="tpu_custom_call", output_to_operand_aliasing={{0}: (8, {})} | custom-call | flops 19595788288 | bytes 4718592 | tf_op jit(solution)/shard_map/pair_backward_1/pallas_call | solution.py:157
  176.4 29.2 %weight_reduce.1 = f32[128,1792]{1,0:T(8,128)} custom-call(f32[128,1792]{1,0:T(8,128)} %get-tuple-element.26.part_ref), custom_call_target="tpu_custom_call" | custom-call | tf_op jit(solution)/shard_map/weight_reduce/pallas_call | solution.py:327
  205.6 0.7 slice.19
  206.3 1.0 slice_bitcast_fusion
  207.2 1.9 slice.17
  209.1 0.6 copy.48
  209.7 0.8 copy.38
Async XLA Ops:
  22.4 28.0 %all-to-all-start.1 = ((bf16[16,2,16,512]{3,2,1,0:T(8,128)(2,1)}), bf16[16,2,16,512]{3,2,1,0:T(8,128)(2,1)S(1)}, u32[]{:S(2)}, u32[]{:S(2)}) async-start(bf16[16,2,16,512]{3,2,1,0:T(8,128)(2,1)} %bitcast.7), calls=%async_computation.1 | async-start | bytes 1048576 | tf_op jit(solution)/shard_map/all_to_all | solution.py:347
  29.8 26.5 %copy-start.2 = (s32[2]{0:T(128)S(1)}, s32[2]{0:T(128)}, u32[]{:S(2)}) copy-start(s32[2]{0:T(128)} %param.15) | copy-start | bytes 28
  50.4 20.3 %all-to-all-start = ((bf16[16,2,16,512]{3,2,1,0:T(8,128)(2,1)}), bf16[16,2,16,512]{3,2,1,0:T(8,128)(2,1)S(1)}, u32[]{:S(2)}, u32[]{:S(2)}) async-start(bf16[16,2,16,512]{3,2,1,0:T(8,128)(2,1)} %bitcast.4), calls=%async_computation | async-start | bytes 1048576 | tf_op jit(solution)/shard_map/all_to_all | solution.py:347
  70.7 19.8 %copy-start.1 = (bf16[512,128]{1,0:T(8,128)(2,1)S(1)}, bf16[512,128]{1,0:T(8,128)(2,1)}, u32[]{:S(2)}) copy-start(bf16[512,128]{1,0:T(8,128)(2,1)} %wout_ref.7) | copy-start | bytes 393220
  70.7 20.6 %copy-start = (bf16[128,1024]{1,0:T(8,128)(2,1)S(1)}, bf16[128,1024]{1,0:T(8,128)(2,1)}, u32[]{:S(2)}) copy-start(bf16[128,1024]{1,0:T(8,128)(2,1)} %win_ref.7) | copy-start | bytes 786436
  86.3 18.4 %all-to-all-start.2 = ((bf16[16,2,16,512]{3,1,2,0:T(2,128)(2,1)}), bf16[16,2,16,512]{3,1,2,0:T(2,128)(2,1)S(1)}, u32[]{:S(2)}, u32[]{:S(2)}) async-start(bf16[16,2,16,512]{3,1,2,0:T(2,128)(2,1)} %bitcast.37), calls=%async_computation.2 | async-start | bytes 1048576 | tf_op jit(solution)/shard_map/all_to_all | solution.py:347
  104.8 37.7 %all-to-all-start.3 = ((bf16[16,2,16,512]{3,1,2,0:T(2,128)(2,1)}), bf16[16,2,16,512]{3,1,2,0:T(2,128)(2,1)S(1)}, u32[]{:S(2)}, u32[]{:S(2)}) async-start(bf16[16,2,16,512]{3,1,2,0:T(2,128)(2,1)} %bitcast.36), calls=%async_computation.3 | async-start | bytes 1048576 | tf_op jit(solution)/shard_map/all_to_all | solution.py:347
